TPU v7x, 32 devices: a whole 2x2x4 slice. The times are simulated.
32 devices in a mesh: row: 4 (over y, core), col: 8 (over z, x).
Axes of the slice: x: 2, y: 2, z: 4, core: 2. Of those that a mesh axis runs over, the one named last changes fastest.
Arguments:
- grads: bfloat16 [1024, 8192], P('row', 'col'), may hold values from -64 to 64
Outputs:
- kernel: float32 [1024, 1024], P('row', 'col')
All inputs are finite; a program needn't handle non-finite values.
Results may differ from a plain program's by a relative error of at most 0.002.
Values may be sent and summed in bfloat16 or wider, within the bound.
No kernel may reach another device: no remote copies, remote signals or barrier semaphores. Data moves between devices by JAX's collectives and lax.ppermute only.
A program may use at most 64 MiB of HBM per device.

v0:
```python
import jax
import jax.numpy as jnp
from jax import lax
from jax.sharding import PartitionSpec as P

K = 8192
BW = 64


def spread(block, axis, owner):
    block = jnp.where(lax.axis_index(axis) == owner, block, jnp.zeros_like(block))
    return lax.psum(block, axis)


def blocked(rows_in):
    count = rows_in.shape[0]
    step = min(count, 128)
    return rows_in.reshape(count // step, step, rows_in.shape[1] // BW, BW)


def layer_fisher(rows_in):
    values = rows_in.reshape(rows_in.shape[0], rows_in.shape[1] // BW, BW)
    return jnp.einsum("nlb,nlc->lbc", values, values, preferred_element_type=jnp.float32)


def factor(total, count):
    width = total.shape[-1]
    unit = jnp.eye(width, dtype=jnp.float32)
    fisher = total / count + 0.1 * unit
    lower = jnp.linalg.cholesky(fisher)
    return jax.vmap(lambda matrix: jax.scipy.linalg.solve_triangular(matrix, unit, lower=True))(
        lower
    )


def whiten(rows_in, inverse):

    def apply_block(block):
        values = block.astype(jnp.float32)
        return jnp.einsum("nlb,lcb->nlc", values, inverse, precision=lax.Precision.HIGHEST).astype(
            jnp.bfloat16
        )

    return lax.map(apply_block, blocked(rows_in)).reshape(rows_in.shape)


def per_device(grads):
    count = grads.shape[0]
    total_count = count * lax.axis_size("row")
    total = lax.psum(layer_fisher(grads), "row")
    features = lax.all_gather(whiten(grads, factor(total, total_count)), "col", axis=1, tiled=True)
    block = count // 2
    column = lax.axis_index("col")
    mine = lax.dynamic_slice_in_dim(features, column % 2 * block, block, 0)
    partner = spread(mine, "row", column // 2)
    scale = K ** (-0.5)

    def product(half):
        left = features[half * block : (half + 1) * block]
        return (
            lax.dot_general(
                left, partner, (((1,), (1,)), ((), ())), preferred_element_type=jnp.float32
            )
            * scale
        )

    return jnp.concatenate([product(0), product(1)], axis=0)


def solution(mesh):
    in_specs = (P("row", "col"),)
    out_specs = P("row", "col")
    return jax.shard_map(
        per_device, mesh=mesh, in_specs=in_specs, out_specs=out_specs, check_vma=False
    )
```

profile of v0, /device:TPU:0, one launch (start us, length us, event | category | flops | bytes accessed | tf_op | source)
XLA Modules:
  0.0 363.0 jit_solution(17992931181714440704)
XLA Ops:
  6.5 0.0 copy-start
  6.5 0.0 all-reduce.3.cloned.1.call-start
  6.5 1.3 copy.17
  7.9 1.1 fusion.21
  8.9 0.0 all-reduce.3.cloned.1.call-update
  9.0 0.0 all-gather.2.cloned.1.call-start
  9.1 0.0 copy-done
  9.1 0.7 reshape.31
  9.7 0.1 copy.19
  9.8 0.9 copy.22
  10.7 35.2 %all-reduce.3.cloned.1.call-done = f32[16,64,64]{1,2,0:T(8,128)} async-done(((f32[16,64,64]{1,2,0:T(8,128)}), f32[16,64,64]{1,2,0:T(8,128)}) %all-reduce.3.cloned.1.call-update) | async-done | bytes 262160 | tf_op jit(solution)/shard_map/psum | solution.py:50
  45.9 0.0 copy-start.1
  45.9 1.2 multiply_add_fusion
  47.0 0.2 copy.20
  47.2 0.0 copy-done.1
  47.2 0.1 fusion.17
  47.3 93.8 %custom-call.8 = f32[16,64,64]{2,1,0:T(8,128)S(1)} custom-call(f32[16,64,64]{2,1,0:T(8,128)S(1)} %fusion.17), custom_call_target="Cholesky" | custom-call | tf_op jit(solution)/shard_map/jit(cholesky)/cholesky | solution.py:30
  141.1 0.1 select_reduce_fusion
  141.2 0.1 compare_reduce_fusion
  141.3 0.1 select_bitcast_fusion
  141.5 78.6 %custom-call.9 = f32[16,1,64,64]{2,3,1,0:T(8,128)S(1)} custom-call(f32[16,1,64,64]{3,2,1,0:T(8,128)S(1)} %select_bitcast_fusion), custom_call_target="InvertDiagBlocksLowerTriangular" | custom-call | tf_op jit(solution)/shard_map/vmap(jit(_solve_triangular))/triangular_solve | solution.py:31
  220.1 1.0 fusion.15
  221.1 0.9 while.10
  221.1 0.4 fusion.32
  221.6 0.4 fusion.32
  222.0 0.5 copy.23
  222.6 0.9 copy.30
  223.4 0.0 all-gather.2.cloned.1.call-update
  223.5 0.0 all-reduce.5.cloned.1.call-start
  223.5 73.0 %all-gather.2.cloned.1.call-done = bf16[256,8192]{0,1:T(8,128)(2,1)} async-done(((bf16[256,1024]{0,1:T(8,128)(2,1)}), bf16[256,8192]{0,1:T(8,128)(2,1)}) %all-gather.2.cloned.1.call-update) | async-done | bytes 4194320 | tf_op jit(solution)/shard_map/all_gather | solution.py:51
  296.5 3.3 dynamic-slice_select_fusion
  299.8 0.0 all-reduce.5.cloned.1.call-update
  299.9 50.1 %all-reduce.5.cloned.1.call-done = bf16[128,8192]{0,1:T(8,128)(2,1)} async-done(((bf16[128,8192]{0,1:T(8,128)(2,1)}), bf16[128,8192]{0,1:T(8,128)(2,1)}) %all-reduce.5.cloned.1.call-update) | async-done | bytes 2097168 | tf_op jit(solution)/shard_map/psum | solution.py:12
  349.9 0.0 copy-start.2
  349.9 3.1 fusion.12
  353.1 0.3 copy-done.2
  353.4 2.4 fusion.9
  355.8 0.7 pad_maximum_fusion
  (5 shorter events, 0.0 us)
Async XLA Ops:
  6.5 2.5 copy-start
  6.5 39.3 %all-reduce.3.cloned.1.call-start = ((), (), s32[]{:S(2)}) async-start(), calls=%async_computation | async-start | bytes 1048576 | tf_op jit(solution)/shard_map/psum | solution.py:50
  9.0 287.5 %all-gather.2.cloned.1.call-start = ((), (), s32[]{:S(2)}) async-start(), calls=%async_computation.1 | async-start | bytes 4718592 | tf_op jit(solution)/shard_map/all_gather | solution.py:51
  45.9 1.4 copy-start.1
  223.5 126.5 %all-reduce.5.cloned.1.call-start = ((), (), s32[]{:S(2)}) async-start(), calls=%async_computation.2 | async-start | bytes 4194304 | tf_op jit(solution)/shard_map/psum | solution.py:12
  349.9 3.4 copy-start.2
Sparse Core Ops, SparseCore 0:
  9.7 36.1 all-reduce.2
  223.6 72.8 all-gather.1
  300.0 49.9 all-reduce.4
where the time goes:
time: 363 us
  other arithmetic  178 us (49%)
  waiting for transfers between devices  158 us (44%)
  between operations  13.3 us (4%)
  matrix products  8.42 us (2%)
  local copies, waits for them, and re-layouts  4.86 us (1%)
    another operation x4, other arithmetic, factor(): lower = jnp.linalg.cholesky(fisher)  94 us
    another operation x3, other arithmetic, factor(): jax.scipy.linalg.solve_triangular(matrix, unit, lower=True)  78.8 us
    all_gather x1, waiting for transfers between devices, per_device(): lax.all_gather(whiten(grads, factor(total, total_count)), 'col', axis=1,...  73 us
    psum x1, waiting for transfers between devices, spread(): return lax.psum(block, axis)  50.1 us
    psum x1, waiting for transfers between devices, per_device(): total = lax.psum(layer_fisher(grads), 'row')  35.2 us
  transfers between devices with their start and end apart: 3, of which 3 were waited for; matrix products, arithmetic and copies ran while one was open for 0% of the time, Pallas kernels for 0%

commit v1 on v0

v1 whole, which is shorter than its diff:
```python
import functools

import jax
import jax.numpy as jnp
from jax import lax
from jax.experimental import pallas as pl
from jax.experimental.pallas import tpu as pltpu
from jax.sharding import PartitionSpec as P

BW = 64
LANES = 128


def lane_gather(rows, index):
    return jnp.take_along_axis(rows, index, axis=1, mode="promise_in_bounds")


def factor(packed):
    groups = packed.shape[0]
    lane = lax.broadcasted_iota(jnp.int32, (groups, LANES), 1)
    base = jnp.where(lane >= BW, BW, 0)
    column = lane - base
    rows = [packed[:, k, :] for k in range(BW)]
    for j in range(BW):
        row = rows[j]
        pivot = lane_gather(row, base + j)
        here = column == j
        step = jnp.where(here, 1.0, row) * (1.0 / pivot)
        for k in range(j + 1, BW):
            rows[k] = jnp.where(here, 0.0, rows[k]) - lane_gather(row, base + k) * step
        packed[:, j, :] = jnp.where(column < j, row, jnp.where(here, 1.0, 0.0)) * lax.rsqrt(pivot)


def body(me_ref, *refs, slots, peers, total):
    grads = refs[:slots]
    outs = refs[slots : slots + peers]
    packed, white = refs[slots + peers :]
    count, width = grads[0].shape
    groups = width // LANES
    block = outs[0].shape[1]

    lane = lax.broadcasted_iota(jnp.int32, (BW, LANES), 1)
    sub = lax.broadcasted_iota(jnp.int32, (BW, LANES), 0)
    low = lane < BW
    unit = jnp.where(sub == jnp.where(low, lane, lane - BW), 0.1, 0.0)
    for s in range(groups):
        acc = None
        for t in range(slots):
            x = grads[t][:, s * LANES : (s + 1) * LANES]
            part = lax.dot_general(
                x, x, (((0,), (0,)), ((), ())), preferred_element_type=jnp.float32
            )
            acc = part if acc is None else acc + part
        packed[s] = jnp.where(low, acc[:BW], acc[BW:]) * (1.0 / total) + unit

    factor(packed)

    for s in range(groups):
        both = packed[s]
        wide = jnp.concatenate([jnp.where(low, both, 0.0), jnp.where(low, 0.0, both)], axis=0)
        high = wide.astype(jnp.bfloat16)
        rest = (wide - high.astype(jnp.float32)).astype(jnp.bfloat16)
        stacked = jnp.concatenate([high, rest], axis=1)
        for t in range(slots):
            x = grads[t][:, s * LANES : (s + 1) * LANES]
            out = lax.dot_general(
                jnp.concatenate([x, x], axis=1),
                stacked,
                (((1,), (1,)), ((), ())),
                preferred_element_type=jnp.float32,
            )
            white[t * count : (t + 1) * count, s * LANES : (s + 1) * LANES] = out.astype(
                jnp.bfloat16
            )

    mine = white[:count, :]
    for p in range(peers):
        start = pl.multiple_of(me_ref[p], block)
        outs[p][...] = lax.dot_general(
            mine,
            white[pl.ds(start, block), :],
            (((1,), (1,)), ((), ())),
            preferred_element_type=jnp.float32,
        ).astype(outs[p].dtype)


def per_device(grads):
    slots = lax.axis_size("row")
    peers = lax.axis_size("col")
    count, width = grads.shape
    total = count * slots
    block = total // peers

    held = {0: grads}
    bit = slots // 2
    while bit:
        for t in list(held):
            held[t ^ bit] = lax.ppermute(
                held[t], "row", [(i, i ^ bit) for i in range(slots)]
            )
        bit //= 2

    row = lax.axis_index("row")
    col = lax.axis_index("col")
    per_slot = count // block
    peer = col ^ jnp.arange(peers, dtype=jnp.int32)
    starts = ((peer // per_slot) ^ row) * count + (peer % per_slot) * block

    outs = pl.pallas_call(
        functools.partial(body, slots=slots, peers=peers, total=total),
        in_specs=[pl.BlockSpec(memory_space=pltpu.SMEM)]
        + [pl.BlockSpec(memory_space=pltpu.VMEM)] * slots,
        out_specs=[pl.BlockSpec(memory_space=pltpu.VMEM)] * peers,
        out_shape=[
            jax.ShapeDtypeStruct((count, block), jnp.bfloat16 if p else jnp.float32)
            for p in range(peers)
        ],
        scratch_shapes=[
            pltpu.VMEM((width // LANES, BW, LANES), jnp.float32),
            pltpu.VMEM((total, width), jnp.bfloat16),
        ],
    )(starts, *[held[t] for t in range(slots)])

    kernel = outs[0]
    for p in range(1, peers):
        got = lax.ppermute(outs[p], "col", [(i, i ^ p) for i in range(peers)])
        kernel = kernel + got.astype(jnp.float32)
    return kernel * (width * peers) ** (-0.5)


def solution(mesh):
    return jax.shard_map(
        per_device,
        mesh=mesh,
        in_specs=(P("row", "col"),),
        out_specs=P("row", "col"),
        check_vma=False,
    )
```

time: 363 us -> 49.1 us (0.14)
  other arithmetic: 178 us -> 2.24 us
  waiting for transfers between devices: 158 us -> 20.7 us
  starting transfers between devices: 0.09 us -> 14.2 us
  between operations: 13.3 us -> 0.02 us
  Pallas kernels: 0 us -> 11 us
  matrix products: 8.42 us -> 0 us
  local copies, waits for them, and re-layouts: 4.86 us -> 0.84 us
    another operation x7 -> x0, other arithmetic: 173 us -> none  [the longest x4 94 us: factor(): lower = jnp.linalg.cholesky(fisher)]
    psum x2 -> x0, waiting for transfers between devices: 85.3 us -> none  [the longest x1 50.1 us: spread(): return lax.psum(block, axis)]
    all_gather x1 -> x0, waiting for transfers between devices: 73 us -> none  [per_device(): lax.all_gather(whiten(grads, factor(total, total_count)), 'col', axis=1,...]
    ppermute x0 -> x10, waiting for transfers between devices: none -> 20.7 us  [the longest x3 13.4 us: per_device(): lax.ppermute(held[t], 'row', [(i, i ^ bit) for i in range(slots)])]
    ppermute x0 -> x10, starting transfers between devices: none -> 14.2 us  [the longest x7 11.2 us: per_device(): got = lax.ppermute(outs[p], 'col', [(i, i ^ p) for i in range(peers)])]
    pallas_call x0 -> x1, Pallas kernels: none -> 11 us  [per_device(): pl.pallas_call(functools.partial(body, slots=slots, peers=peers, total=to...]
    dot_general x5 -> x0, matrix products: 7.41 us -> none  [the longest x2 5.49 us: product(): lax.dot_general(left, partner, (((1,), (1,)), ((), ())), preferred_elemen...]
  transfers between devices with their start and end apart: 3 -> 10, of which waited for: 3 -> 4; matrix products, arithmetic and copies ran while one was open for 0% -> 1% of each run, Pallas kernels for 0% -> 0%
where the time goes in v1:
time: 49.1 us; the launch traced here: 48.9 us
  waiting for transfers between devices  20.7 us (42%)
  starting transfers between devices  14.2 us (29%)
  Pallas kernels  11 us (22%)
  other arithmetic  2.24 us (5%)
  local copies, waits for them, and re-layouts  0.84 us (2%)
    ppermute x3, waiting for transfers between devices, per_device(): lax.ppermute(held[t], 'row', [(i, i ^ bit) for i in range(slots)])  13.4 us
    ppermute x7, starting transfers between devices, per_device(): got = lax.ppermute(outs[p], 'col', [(i, i ^ p) for i in range(peers)])  11.2 us
    pallas_call x1, Pallas kernels, per_device(): pl.pallas_call(functools.partial(body, slots=slots, peers=peers, total=to...  11 us
    ppermute x7, waiting for transfers between devices, per_device(): got = lax.ppermute(outs[p], 'col', [(i, i ^ p) for i in range(peers)])  7.24 us
    ppermute x3, starting transfers between devices, per_device(): lax.ppermute(held[t], 'row', [(i, i ^ bit) for i in range(slots)])  3 us
    mul x1, other arithmetic, per_device(): return kernel * (width * peers) ** (-0.5)  1.63 us
  transfers between devices with their start and end apart: 10, of which 4 were waited for; matrix products, arithmetic and copies ran while one was open for 1% of the time, Pallas kernels for 0%

profile of v1, /device:TPU:0, one launch (start us, length us, event | category | flops | bytes accessed | tf_op | source)
XLA Modules:
  0.0 48.9 jit_solution(17387712251849348703)
XLA Ops:
  0.0 3.0 %collective-permute-start.1 = (bf16[256,1024]{1,0:T(8,128)(2,1)}, bf16[256,1024]{1,0:T(8,128)(2,1)S(1)}, u32[]{:S(2)}, u32[]{:S(2)}) collective-permute-start(bf16[256,1024]{1,0:T(8,128)(2,1)} %refs_0_.1), channel_id=1, source_target_pairs={{0,16},{8,24},{16,0},{24,8},{1,17},{9,25},{17,1},{25,9},{2,18},{10... | collective-permute-start | bytes 1572872 | tf_op jit(solution)/shard_map/ppermute | solution.py:98
  3.0 0.0 collective-permute-start
  3.0 12.1 %collective-permute-done.1.refs_2_ = bf16[256,1024]{1,0:T(8,128)(2,1)S(1)} collective-permute-done((bf16[256,1024]{1,0:T(8,128)(2,1)}, bf16[256,1024]{1,0:T(8,128)(2,1)S(1)}, u32[]{:S(2)}, u32[]{:S(2)}) %collective-permute-start.1) | collective-permute-done | bytes 524320 | tf_op jit(solution)/shard_map/ppermute | solution.py:98
  15.1 0.0 copy-start
  15.1 0.0 collective-permute-start.2
  15.1 0.6 %fusion.1.me_ref = s32[8]{0:T(128)} fusion(s32[]{:T(128)S(6)} %axis_index.25, s32[]{:T(128)S(6)} %axis_index.22), kind=kLoop, calls=%fused_computation.7 | loop fusion | flops 192 | bytes 40 | tf_op jit(solution)/shard_map/add | solution.py:107
  15.7 0.0 collective-permute-done.refs_1_
  15.7 0.0 copy-start.1
  15.7 1.3 %collective-permute-done.2.refs_3_ = bf16[256,1024]{1,0:T(8,128)(2,1)S(1)} collective-permute-done((bf16[256,1024]{1,0:T(8,128)(2,1)S(1)}, bf16[256,1024]{1,0:T(8,128)(2,1)S(1)}, u32[]{:S(2)}, u32[]{:S(2)}) %collective-permute-start.2) | collective-permute-done | bytes 524320 | tf_op jit(solution)/shard_map/ppermute | solution.py:98
  17.0 0.0 copy-done
  17.0 0.0 copy-done.1
  17.0 0.0 copy-start.2
  17.0 0.8 %copy-done.2 = bf16[256,1024]{1,0:T(8,128)(2,1)} copy-done((bf16[256,1024]{1,0:T(8,128)(2,1)}, bf16[256,1024]{1,0:T(8,128)(2,1)S(1)}, u32[]{:S(2)}) %copy-start.2) | copy-done | bytes 524312
  17.9 11.0 %shard_map.17 = (f32[256,128]{1,0:T(8,128)}, bf16[256,128]{1,0:T(8,128)(2,1)}, bf16[256,128]{1,0:T(8,128)(2,1)}, bf16[256,128]{1,0:T(8,128)(2,1)}, bf16[256,128]...) custom-call(s32[8]{0:T(128)} %fusion.1.me_ref, ...), custom_call_target="tpu_custom_call" | custom-call | tf_op jit(solution)/shard_map/pallas_call | solution.py:109
  28.8 1.7 %collective-permute-start.3 = (bf16[256,128]{1,0:T(8,128)(2,1)}, bf16[256,128]{1,0:T(8,128)(2,1)S(1)}, u32[]{:S(2)}, u32[]{:S(2)}) collective-permute-start(bf16[256,128]{1,0:T(8,128)(2,1)} %get-tuple-element.14), channel_id=1, source_target_pairs={{0,1},{1,0},{2,3},{3,2},{4,5},{5,4},{6,7},{7,6},{8,9},{9,8},{10,11... | collective-permute-start | bytes 196616 | tf_op jit(solution)/shard_map/ppermute | solution.py:126
  30.5 1.6 %collective-permute-start.4 = (bf16[256,128]{1,0:T(8,128)(2,1)}, bf16[256,128]{1,0:T(8,128)(2,1)S(1)}, u32[]{:S(2)}, u32[]{:S(2)}) collective-permute-start(bf16[256,128]{1,0:T(8,128)(2,1)} %get-tuple-element.15), channel_id=1, source_target_pairs={{0,2},{1,3},{2,0},{3,1},{4,6},{5,7},{6,4},{7,5},{8,10},{9,11},{10,... | collective-permute-start | bytes 196616 | tf_op jit(solution)/shard_map/ppermute | solution.py:126
  32.1 0.2 collective-permute-start.5
  32.3 2.8 %collective-permute-start.6 = (bf16[256,128]{1,0:T(8,128)(2,1)}, bf16[256,128]{1,0:T(8,128)(2,1)S(1)}, u32[]{:S(2)}, u32[]{:S(2)}) collective-permute-start(bf16[256,128]{1,0:T(8,128)(2,1)} %get-tuple-element.17), channel_id=1, source_target_pairs={{0,4},{1,5},{2,6},{3,7},{4,0},{5,1},{6,2},{7,3},{8,12},{9,13},{10,... | collective-permute-start | bytes 196616 | tf_op jit(solution)/shard_map/ppermute | solution.py:126
  35.1 1.3 %collective-permute-start.7 = (bf16[256,128]{1,0:T(8,128)(2,1)}, bf16[256,128]{1,0:T(8,128)(2,1)S(1)}, u32[]{:S(2)}, u32[]{:S(2)}) collective-permute-start(bf16[256,128]{1,0:T(8,128)(2,1)} %get-tuple-element.18), channel_id=1, source_target_pairs={{0,5},{1,4},{2,7},{3,6},{4,1},{5,0},{6,3},{7,2},{8,13},{9,12},{10,... | collective-permute-start | bytes 196616 | tf_op jit(solution)/shard_map/ppermute | solution.py:126
  36.4 0.0 collective-permute-done.3
  36.4 3.6 %collective-permute-start.8 = (bf16[256,128]{1,0:T(8,128)(2,1)}, bf16[256,128]{1,0:T(8,128)(2,1)S(1)}, u32[]{:S(2)}, u32[]{:S(2)}) collective-permute-start(bf16[256,128]{1,0:T(8,128)(2,1)} %get-tuple-element.19), channel_id=1, source_target_pairs={{0,6},{1,7},{2,4},{3,5},{4,2},{5,3},{6,0},{7,1},{8,14},{9,15},{10,... | collective-permute-start | bytes 196616 | tf_op jit(solution)/shard_map/ppermute | solution.py:126
  40.0 0.0 collective-permute-done.4
  40.0 0.0 collective-permute-start.9
  40.0 0.0 collective-permute-done.5
  40.1 0.0 collective-permute-done.6
  40.1 5.7 %collective-permute-done.7 = bf16[256,128]{1,0:T(8,128)(2,1)S(1)} collective-permute-done((bf16[256,128]{1,0:T(8,128)(2,1)}, bf16[256,128]{1,0:T(8,128)(2,1)S(1)}, u32[]{:S(2)}, u32[]{:S(2)}) %collective-permute-start.7) | collective-permute-done | bytes 65568 | tf_op jit(solution)/shard_map/ppermute | solution.py:126
  45.8 0.0 collective-permute-done.8
  45.8 1.5 %collective-permute-done.9 = bf16[256,128]{1,0:T(8,128)(2,1)S(1)} collective-permute-done((bf16[256,128]{1,0:T(8,128)(2,1)}, bf16[256,128]{1,0:T(8,128)(2,1)S(1)}, u32[]{:S(2)}, u32[]{:S(2)}) %collective-permute-start.9) | collective-permute-done | bytes 65568 | tf_op jit(solution)/shard_map/ppermute | solution.py:126
  47.3 1.6 %add_multiply_fusion = f32[256,128]{1,0:T(8,128)} fusion(bf16[256,128]{1,0:T(8,128)(2,1)S(1)} %collective-permute-done.9, bf16[256,128]{1,0:T(8,128)(2,1)S(1)} %collective-permute-done.8, bf16[256,128]{1,0:T(8,128)(2,1)S(1)} %collective-permute-done.7, bf16[256,128]{1,0:T(8,128)(2,1)S(1)} %collective-permute-done.6, ...), kind=kLoop, calls=%fused_computation | loop fusion | flops 491520 | bytes 720896 | tf_op jit(solution)/shard_map/mul | solution.py:128
Async XLA Ops:
  0.0 15.1 %collective-permute-start.1 = (bf16[256,1024]{1,0:T(8,128)(2,1)}, bf16[256,1024]{1,0:T(8,128)(2,1)S(1)}, u32[]{:S(2)}, u32[]{:S(2)}) collective-permute-start(bf16[256,1024]{1,0:T(8,128)(2,1)} %refs_0_.1), channel_id=1, source_target_pairs={{0,16},{8,24},{16,0},{24,8},{1,17},{9,25},{17,1},{25,9},{2,18},{10... | collective-permute-start | bytes 1572872 | tf_op jit(solution)/shard_map/ppermute | solution.py:98
  3.0 12.7 %collective-permute-start = (bf16[256,1024]{1,0:T(8,128)(2,1)}, bf16[256,1024]{1,0:T(8,128)(2,1)S(1)}, u32[]{:S(2)}, u32[]{:S(2)}) collective-permute-start(bf16[256,1024]{1,0:T(8,128)(2,1)} %refs_0_.1), channel_id=1, source_target_pairs={{0,8},{8,0},{16,24},{24,16},{1,9},{9,1},{17,25},{25,17},{2,10},{10... | collective-permute-start | bytes 1572872 | tf_op jit(solution)/shard_map/ppermute | solution.py:98
  15.1 1.9 %copy-start = (bf16[256,1024]{1,0:T(8,128)(2,1)}, bf16[256,1024]{1,0:T(8,128)(2,1)S(1)}, u32[]{:S(2)}) copy-start(bf16[256,1024]{1,0:T(8,128)(2,1)S(1)} %collective-permute-done.1.refs_2_) | copy-start | bytes 1572868
  15.1 1.9 %collective-permute-start.2 = (bf16[256,1024]{1,0:T(8,128)(2,1)S(1)}, bf16[256,1024]{1,0:T(8,128)(2,1)S(1)}, u32[]{:S(2)}, u32[]{:S(2)}) collective-permute-start(bf16[256,1024]{1,0:T(8,128)(2,1)S(1)} %collective-permute-done.1.refs_2_), channel_id=1, source_target_pairs={{0,8},{8,0},{16,24},{24,16},{1,9},{9,1},{17,25},{25,17},{2,10},{10... | collective-permute-start | bytes 1572872 | tf_op jit(solution)/shard_map/ppermute | solution.py:98
  15.7 1.3 %copy-start.1 = (bf16[256,1024]{1,0:T(8,128)(2,1)}, bf16[256,1024]{1,0:T(8,128)(2,1)S(1)}, u32[]{:S(2)}) copy-start(bf16[256,1024]{1,0:T(8,128)(2,1)S(1)} %collective-permute-done.refs_1_) | copy-start | bytes 1572868
  17.0 0.8 %copy-start.2 = (bf16[256,1024]{1,0:T(8,128)(2,1)}, bf16[256,1024]{1,0:T(8,128)(2,1)S(1)}, u32[]{:S(2)}) copy-start(bf16[256,1024]{1,0:T(8,128)(2,1)S(1)} %collective-permute-done.2.refs_3_) | copy-start | bytes 1572868
  28.8 7.6 %collective-permute-start.3 = (bf16[256,128]{1,0:T(8,128)(2,1)}, bf16[256,128]{1,0:T(8,128)(2,1)S(1)}, u32[]{:S(2)}, u32[]{:S(2)}) collective-permute-start(bf16[256,128]{1,0:T(8,128)(2,1)} %get-tuple-element.14), channel_id=1, source_target_pairs={{0,1},{1,0},{2,3},{3,2},{4,5},{5,4},{6,7},{7,6},{8,9},{9,8},{10,11... | collective-permute-start | bytes 196616 | tf_op jit(solution)/shard_map/ppermute | solution.py:126
  30.5 9.5 %collective-permute-start.4 = (bf16[256,128]{1,0:T(8,128)(2,1)}, bf16[256,128]{1,0:T(8,128)(2,1)S(1)}, u32[]{:S(2)}, u32[]{:S(2)}) collective-permute-start(bf16[256,128]{1,0:T(8,128)(2,1)} %get-tuple-element.15), channel_id=1, source_target_pairs={{0,2},{1,3},{2,0},{3,1},{4,6},{5,7},{6,4},{7,5},{8,10},{9,11},{10,... | collective-permute-start | bytes 196616 | tf_op jit(solution)/shard_map/ppermute | solution.py:126
  32.1 7.9 %collective-permute-start.5 = (bf16[256,128]{1,0:T(8,128)(2,1)}, bf16[256,128]{1,0:T(8,128)(2,1)S(1)}, u32[]{:S(2)}, u32[]{:S(2)}) collective-permute-start(bf16[256,128]{1,0:T(8,128)(2,1)} %get-tuple-element.16), channel_id=1, source_target_pairs={{0,3},{1,2},{2,1},{3,0},{4,7},{5,6},{6,5},{7,4},{8,11},{9,10},{10,... | collective-permute-start | bytes 196616 | tf_op jit(solution)/shard_map/ppermute | solution.py:126
  32.3 7.7 %collective-permute-start.6 = (bf16[256,128]{1,0:T(8,128)(2,1)}, bf16[256,128]{1,0:T(8,128)(2,1)S(1)}, u32[]{:S(2)}, u32[]{:S(2)}) collective-permute-start(bf16[256,128]{1,0:T(8,128)(2,1)} %get-tuple-element.17), channel_id=1, source_target_pairs={{0,4},{1,5},{2,6},{3,7},{4,0},{5,1},{6,2},{7,3},{8,12},{9,13},{10,... | collective-permute-start | bytes 196616 | tf_op jit(solution)/shard_map/ppermute | solution.py:126
  35.1 10.7 %collective-permute-start.7 = (bf16[256,128]{1,0:T(8,128)(2,1)}, bf16[256,128]{1,0:T(8,128)(2,1)S(1)}, u32[]{:S(2)}, u32[]{:S(2)}) collective-permute-start(bf16[256,128]{1,0:T(8,128)(2,1)} %get-tuple-element.18), channel_id=1, source_target_pairs={{0,5},{1,4},{2,7},{3,6},{4,1},{5,0},{6,3},{7,2},{8,13},{9,12},{10,... | collective-permute-start | bytes 196616 | tf_op jit(solution)/shard_map/ppermute | solution.py:126
  36.4 9.4 %collective-permute-start.8 = (bf16[256,128]{1,0:T(8,128)(2,1)}, bf16[256,128]{1,0:T(8,128)(2,1)S(1)}, u32[]{:S(2)}, u32[]{:S(2)}) collective-permute-start(bf16[256,128]{1,0:T(8,128)(2,1)} %get-tuple-element.19), channel_id=1, source_target_pairs={{0,6},{1,7},{2,4},{3,5},{4,2},{5,3},{6,0},{7,1},{8,14},{9,15},{10,... | collective-permute-start | bytes 196616 | tf_op jit(solution)/shard_map/ppermute | solution.py:126
  40.0 7.3 %collective-permute-start.9 = (bf16[256,128]{1,0:T(8,128)(2,1)}, bf16[256,128]{1,0:T(8,128)(2,1)S(1)}, u32[]{:S(2)}, u32[]{:S(2)}) collective-permute-start(bf16[256,128]{1,0:T(8,128)(2,1)} %get-tuple-element.20), channel_id=1, source_target_pairs={{0,7},{1,6},{2,5},{3,4},{4,3},{5,2},{6,1},{7,0},{8,15},{9,14},{10,... | collective-permute-start | bytes 196616 | tf_op jit(solution)/shard_map/ppermute | solution.py:126
